TPU v7x, 32 devices: a whole 2x2x4 slice. The times are simulated.
32 devices in a mesh: shard: 8 (over y, x, core), ctx: 4 (over z).
Axes of the slice: x: 2, y: 2, z: 4, core: 2. Of those that a mesh axis runs over, the one named last changes fastest.
Arguments:
- hidden_in: float32 [8, 1024, 1024], P('shard', 'ctx'), may hold values from -6 to 6
- mixer_gain: float32 [1024], replicated, may hold values from 0.5 to 1.5
- mixer_proj: bfloat16 [1024, 3072], P(('shard', 'ctx')), may hold values from -0.1875 to 0.1875
- decay_proj: bfloat16 [1024, 8], P(('shard', 'ctx')), may hold values from -0.1875 to 0.1875
- conv_kernel: float32 [4, 2048], replicated, may hold values from -3 to 3
- decay_log: float32 [4], replicated, may hold values from -1 to 1
- decay_bias: float32 [4], replicated, may hold values from -7 to -2
- output_gain: float32 [256], replicated, may hold values from 0.5 to 1.5
- mixer_out: bfloat16 [1024, 1024], P(('shard', 'ctx')), may hold values from -0.375 to 0.375
- ffn_gain: float32 [1024], replicated, may hold values from 0.5 to 1.5
- ffn_up: bfloat16 [2, 2816, 1024], P(None, ('shard', 'ctx')), may hold values from -0.1875 to 0.1875
- ffn_down: bfloat16 [2816, 1024], P(('shard', 'ctx')), may hold values from -0.109375 to 0.109375
- cotangent: float32 [8, 1024, 1024], P('shard', 'ctx'), may hold values from -6 to 6
Outputs:
- block_out: float32 [8, 1024, 1024], P('shard', 'ctx')
- input_grad: float32 [8, 1024, 1024], P('shard', 'ctx')
- mixer_gain_grad: float32 [1024], replicated
- mixer_proj_grad: float32 [1024, 3072], P(('shard', 'ctx'))
- decay_proj_grad: float32 [1024, 8], P(('shard', 'ctx'))
- conv_kernel_grad: float32 [4, 2048], replicated
- decay_log_grad: float32 [4], replicated
- decay_bias_grad: float32 [4], replicated
- output_gain_grad: float32 [256], replicated
- mixer_out_grad: float32 [1024, 1024], P(('shard', 'ctx'))
- ffn_gain_grad: float32 [1024], replicated
- ffn_up_grad: float32 [2, 2816, 1024], P(None, ('shard', 'ctx'))
- ffn_down_grad: float32 [2816, 1024], P(('shard', 'ctx'))
All inputs are finite; a program needn't handle non-finite values.
Results may differ from a plain program's by a relative error of at most 0.025.
The roundings to bfloat16 on the way count: a program that leaves them out, or rounds other values in their place, can miss the bound.
Values may be sent and summed in bfloat16 or wider, within the bound.
A program may use at most 192 MiB of HBM per device.

v0:
```python
import jax
import jax.numpy as jnp
from jax import lax
from jax.sharding import PartitionSpec as P

H = 4
DK = 128
DV = 256
CONV = 4
BLOCK = 64
QK = 512
VV = 1024


norm_eps = 1e-06
exact_mode = lax.Precision.HIGHEST


def shifted(shard, axis, by):
    devices = lax.axis_size(axis)
    pairs = [(i, i + by) for i in range(devices) if 0 <= i + by < devices]
    return lax.ppermute(shard, axis, pairs)


def carried_in(shard, axis, join, neutral):
    place = lax.axis_index(axis)
    gathered = jax.tree.map(
        lambda a, kind: lax.all_gather(a.astype(kind), axis), shard, (jnp.bfloat16, jnp.bfloat16)
    )
    state = jax.tree.map(lambda a, e: jnp.zeros_like(a) + jnp.asarray(e, a.dtype), shard, neutral)

    def one(step, state):
        return join(
            state,
            jax.tree.map(
                lambda a, own: lax.dynamic_index_in_dim(a, step, 0, False).astype(own.dtype),
                gathered,
                shard,
            ),
        )

    return lax.fori_loop(0, place, one, state)


def carried_in_2(shard, axis, combine, identity):
    devices, place = (lax.axis_size(axis), lax.axis_index(axis))
    everything = jax.tree.map(
        lambda part, kind: lax.all_gather(part.astype(kind), axis),
        shard,
        jax.tree.map(lambda a: jnp.bfloat16 if a.dtype == jnp.float32 else a.dtype, shard),
    )
    start = jax.tree.map(
        lambda part, zero: jnp.broadcast_to(jnp.asarray(zero, part.dtype), part.shape),
        shard,
        identity,
    )

    def step(k, before):
        at = devices - 1 - k
        reached = at > place
        new = combine(
            before, jax.tree.map(lambda part, own: part[at].astype(own.dtype), everything, shard)
        )
        return jax.tree.map(lambda a, b: jnp.where(reached, a, b), new, before)

    return lax.fori_loop(0, devices, step, start)


def block_step(carry_state, queries, keys_in, values_in, decays, beta_in):
    size = decays.shape[-1]
    cumul = jnp.cumsum(decays, axis=-1)
    later = jnp.arange(size)[:, None]
    earlier = jnp.arange(size)[None, :]
    strict = earlier < later
    inclusive = earlier <= later
    spread = cumul[..., :, None] - cumul[..., None, :]
    decay_strict = jnp.where(strict, jnp.exp(jnp.where(strict, spread, 0.0)), 0.0)
    decay_incl = jnp.where(inclusive, jnp.exp(jnp.where(inclusive, spread, 0.0)), 0.0)
    key_key = jnp.einsum("bhtk,bhsk->bhts", keys_in, keys_in, precision=exact_mode)
    query_key = jnp.einsum("bhtk,bhsk->bhts", queries, keys_in, precision=exact_mode)
    lower_mat = jnp.eye(size, dtype=jnp.float32) + beta_in[..., :, None] * decay_strict * key_key
    growth = jnp.exp(cumul)
    seen = jnp.einsum("bhtk,bhkw->bhtw", keys_in, carry_state, precision=exact_mode)
    right_side = beta_in[..., None] * (values_in - growth[..., None] * seen)
    deltas = jax.scipy.linalg.solve_triangular(lower_mat, right_side, lower=True)
    from_state = jnp.einsum("bhtk,bhkw->bhtw", queries, carry_state, precision=exact_mode)
    outputs = growth[..., None] * from_state + jnp.einsum(
        "bhts,bhsw->bhtw", query_key * decay_incl, deltas, precision=exact_mode
    )
    tail_decay = jnp.exp(cumul[..., -1:] - cumul)
    new_state = jnp.exp(cumul[..., -1])[..., None, None] * carry_state + jnp.einsum(
        "bhsk,bhsw->bhkw", keys_in * tail_decay[..., None], deltas, precision=exact_mode
    )
    return (new_state, outputs)


def to_blocks(array):
    seq_count, length = (array.shape[0], array.shape[1])
    shaped = array.reshape((seq_count, length // BLOCK, BLOCK) + array.shape[2:])
    if shaped.ndim == 5:
        return shaped.transpose(1, 0, 3, 2, 4)
    return shaped.transpose(1, 0, 3, 2)


def run_blocks(start_state, queries, keys_in, values_in, decays, beta_in):
    seq_count, length = (decays.shape[0], decays.shape[1])

    def advance(carry_state, item):
        return block_step(carry_state, item[0], item[1], item[2], item[3], item[4])

    final_state, outputs = lax.scan(
        advance,
        start_state,
        (
            to_blocks(queries),
            to_blocks(keys_in),
            to_blocks(values_in),
            to_blocks(decays),
            to_blocks(beta_in),
        ),
    )
    outputs = outputs.transpose(1, 0, 3, 2, 4).reshape(seq_count, length, H, outputs.shape[-1])
    return (final_state, outputs)


def conv_silu(padded, kernel):
    length = padded.shape[1] - (CONV - 1)
    total = kernel[0] * padded[:, 0:length]
    for offset in range(1, CONV):
        total = total + kernel[offset] * padded[:, offset : offset + length]
    return jax.nn.silu(total)


def split_heads(act, rate_in, decay_log, decay_bias):
    seq_count, length = (act.shape[0], act.shape[1])
    query_raw = act[..., :QK].reshape(seq_count, length, H, DK)
    key_raw = act[..., QK : 2 * QK].reshape(seq_count, length, H, DK)
    values_in = act[..., 2 * QK :].reshape(seq_count, length, H, DV)
    queries = (
        query_raw
        * lax.rsqrt(jnp.sum(query_raw * query_raw, -1, keepdims=True) + norm_eps)
        * DK ** (-0.5)
    )
    keys_in = key_raw * lax.rsqrt(jnp.sum(key_raw * key_raw, -1, keepdims=True) + norm_eps)
    decays = -jnp.exp(decay_log) * jax.nn.softplus(rate_in[..., :H] + decay_bias)
    beta_in = jax.nn.sigmoid(rate_in[..., H:])
    return (queries, keys_in, values_in, decays, beta_in)


def gate_norm(mixed_out, gate_pre, output_gain):
    seq_count, length = (gate_pre.shape[0], gate_pre.shape[1])
    gate_heads = gate_pre.reshape(seq_count, length, H, DV)
    scaled = mixed_out * lax.rsqrt(jnp.mean(mixed_out * mixed_out, -1, keepdims=True) + norm_eps)
    return (scaled * output_gain * jax.nn.silu(gate_heads)).reshape(seq_count, length, H * DV)


def local_core(padded, rate_in, kernel, decay_log, decay_bias):
    act = conv_silu(padded, kernel)
    queries, keys_in, values_in, decays, beta_in = split_heads(act, rate_in, decay_log, decay_bias)
    seq_count, length = (decays.shape[0], decays.shape[1])
    values_aug = jnp.concatenate(
        [values_in, jnp.zeros((seq_count, length, H, DK), jnp.float32)], -1
    )
    start_state = jnp.concatenate(
        [
            jnp.zeros((seq_count, H, DK, DV), jnp.float32),
            jnp.broadcast_to(jnp.eye(DK, dtype=jnp.float32), (seq_count, H, DK, DK)),
        ],
        -1,
    )
    final_state, outputs = run_blocks(start_state, queries, keys_in, values_aug, decays, beta_in)
    return (outputs[..., :DV], outputs[..., DV:], final_state[..., :DV], final_state[..., DV:])


def correct_norm(local_out, query_map, state_in, gate_pre, output_gain):
    mixed_out = local_out + jnp.einsum("bthk,bhkw->bthw", query_map, state_in, precision=exact_mode)
    return gate_norm(mixed_out, gate_pre, output_gain)


def compose(earlier, later):
    return (
        jnp.einsum("bhij,bhjk->bhik", later[0], earlier[0], precision=exact_mode),
        jnp.einsum("bhij,bhjw->bhiw", later[0], earlier[1], precision=exact_mode) + later[1],
    )


def rms_back(inputs, scale, gain, upstream):
    unit = inputs * scale
    weighted = upstream * gain
    gain_grad = jnp.sum(upstream * unit, axis=0)
    return (scale * (weighted - unit * jnp.mean(weighted * unit, -1, keepdims=True)), gain_grad)


def own_features(rows, shard_count, ctx_count, ctx_place):
    width = rows.shape[-1]
    piece = width // (shard_count * ctx_count)
    shaped = rows.reshape(rows.shape[:-1] + (shard_count, ctx_count, piece))
    taken = lax.dynamic_index_in_dim(shaped, ctx_place, rows.ndim, keepdims=False)
    return taken.reshape(rows.shape[:-1] + (shard_count * piece,))


def ffn_local(ffn_rows, cot_rows, up_weight, down_weight):
    up_one = jnp.dot(ffn_rows, up_weight[0].T, preferred_element_type=jnp.float32)
    up_two = jnp.dot(ffn_rows, up_weight[1].T, preferred_element_type=jnp.float32)
    sigma = jax.nn.sigmoid(up_one)
    activ = (up_one * sigma * up_two).astype(jnp.bfloat16)
    ffn_part = jnp.dot(activ, down_weight, preferred_element_type=jnp.float32)
    d_activ = jnp.dot(cot_rows, down_weight.T, preferred_element_type=jnp.float32)
    d_one = (d_activ * up_two * sigma * (1.0 + up_one * (1.0 - sigma))).astype(jnp.bfloat16)
    d_two = (d_activ * up_one * sigma).astype(jnp.bfloat16)
    down_grad = jnp.dot(activ.T, cot_rows, preferred_element_type=jnp.float32)
    up_grad = jnp.stack(
        [
            jnp.dot(d_one.T, ffn_rows, preferred_element_type=jnp.float32),
            jnp.dot(d_two.T, ffn_rows, preferred_element_type=jnp.float32),
        ]
    )
    d_input = jnp.dot(d_one, up_weight[0], preferred_element_type=jnp.float32) + jnp.dot(
        d_two, up_weight[1], preferred_element_type=jnp.float32
    )
    return (ffn_part, d_input, up_grad, down_grad)


def local(
    hidden_in,
    mixer_gain,
    mixer_proj,
    decay_proj,
    conv_kernel,
    decay_log,
    decay_bias,
    output_gain,
    mixer_out,
    ffn_gain,
    ffn_up,
    ffn_down,
    cotangent,
):
    seq_count, blk_len, feat_dim = hidden_in.shape
    tok_rows = seq_count * blk_len
    conv_width = 2 * QK + VV
    proj_cols = 2 * QK + 2 * VV
    flat_in = hidden_in.reshape(tok_rows, feat_dim)
    scale_in = lax.rsqrt(jnp.mean(flat_in * flat_in, -1, keepdims=True) + norm_eps)
    normed = (flat_in * scale_in * mixer_gain).astype(jnp.bfloat16)
    cot_flat = cotangent.reshape(tok_rows, feat_dim)
    cot_rows = cot_flat.astype(jnp.bfloat16)
    shard_count = lax.axis_size("shard")
    ctx_count = lax.axis_size("ctx")
    ctx_place = lax.axis_index("ctx")
    w_proj, w_rates, up_weight, down_weight = (
        lax.all_gather(mixer_proj, "shard", axis=0, tiled=True),
        lax.all_gather(decay_proj, "shard", axis=0, tiled=True),
        lax.all_gather(ffn_up, "shard", axis=1, tiled=True),
        lax.all_gather(ffn_down, "shard", axis=0, tiled=True),
    )
    w_out = lax.all_gather(mixer_out, ("shard", "ctx"), axis=0, tiled=True)
    all_normed, all_cot = (
        lax.all_gather(normed.reshape(seq_count, blk_len, feat_dim), "ctx", axis=1, tiled=True),
        lax.all_gather(cot_rows.reshape(seq_count, blk_len, feat_dim), "ctx", axis=1, tiled=True),
    )
    rows_sub = own_features(all_normed, shard_count, ctx_count, ctx_place).reshape(
        -1, w_proj.shape[0]
    )
    part_proj = jnp.dot(rows_sub, w_proj, preferred_element_type=jnp.float32).reshape(
        seq_count, -1, proj_cols
    )
    part_rates = jnp.dot(rows_sub, w_rates, preferred_element_type=jnp.float32).reshape(
        seq_count, -1, 2 * H
    )
    proj_sum, rate_in = (
        lax.psum_scatter(part_proj, "ctx", scatter_dimension=1, tiled=True),
        lax.psum_scatter(part_rates, "ctx", scatter_dimension=1, tiled=True),
    )
    projected = proj_sum.reshape(tok_rows, proj_cols)
    pre_rows = projected[:, :conv_width].reshape(seq_count, blk_len, conv_width)
    gate_pre = projected[:, conv_width:].reshape(seq_count, blk_len, VV)
    edge_rows = shifted(pre_rows[:, blk_len - (CONV - 1) :], "ctx", 1)
    padded = jnp.concatenate([edge_rows, pre_rows], 1)
    (local_out, query_map, state_part, state_map), core_back = jax.vjp(
        local_core, padded, rate_in, conv_kernel, decay_log, decay_bias
    )
    identity = (
        jnp.broadcast_to(jnp.eye(DK, dtype=jnp.float32), state_map.shape),
        jnp.zeros_like(state_part),
    )
    prefix = carried_in((state_map, state_part), "ctx", compose, identity)
    state_in = prefix[1]
    gated_out, norm_back = jax.vjp(
        correct_norm, local_out, query_map, state_in, gate_pre, output_gain
    )
    gated_rows = gated_out.reshape(tok_rows, VV).astype(jnp.bfloat16)
    residual = flat_in + jnp.dot(gated_rows, w_out, preferred_element_type=jnp.float32)
    scale_mid = lax.rsqrt(jnp.mean(residual * residual, -1, keepdims=True) + norm_eps)
    ffn_rows = (residual * scale_mid * ffn_gain).astype(jnp.bfloat16)
    all_rows, gated_all = (
        lax.all_gather(ffn_rows.reshape(seq_count, blk_len, feat_dim), "ctx", axis=1, tiled=True),
        lax.all_gather(gated_rows.reshape(seq_count, blk_len, VV), "ctx", axis=1, tiled=True),
    )
    ffn_part, d_input, up_grad, down_grad = ffn_local(
        all_rows.reshape(-1, feat_dim), all_cot.reshape(-1, feat_dim), up_weight, down_weight
    )
    ffn_sum, d_ffn = (
        lax.psum_scatter(
            ffn_part.reshape(seq_count, -1, feat_dim).astype(jnp.bfloat16),
            "ctx",
            scatter_dimension=1,
            tiled=True,
        ).astype(jnp.float32),
        lax.psum_scatter(
            d_input.reshape(seq_count, -1, feat_dim).astype(jnp.bfloat16),
            "ctx",
            scatter_dimension=1,
            tiled=True,
        ).astype(jnp.float32),
    )
    ffn_sum = ffn_sum.reshape(tok_rows, feat_dim)
    d_ffn = d_ffn.reshape(tok_rows, feat_dim)
    block_out = residual + ffn_sum
    d_res_part, gain_two_grad = rms_back(residual, scale_mid, ffn_gain, d_ffn)
    d_residual = cot_flat + d_res_part
    d_res_rows = d_residual.astype(jnp.bfloat16)
    d_gated = jnp.dot(d_res_rows, w_out.T, preferred_element_type=jnp.float32).reshape(
        seq_count, blk_len, VV
    )
    d_local, d_query_map, d_state_in, d_gate, gain_out_grad = norm_back(d_gated)
    suffix = carried_in_2((jnp.swapaxes(state_map, -1, -2), d_state_in), "ctx", compose, identity)
    d_state_out = suffix[1]
    d_map = jnp.einsum("bhiw,bhjw->bhij", d_state_out, state_in, precision=exact_mode)
    d_padded, d_rate, kernel_grad, log_grad, bias_grad = core_back(
        (d_local, d_query_map, d_state_out, d_map)
    )
    d_edge = shifted(d_padded[:, : CONV - 1], "ctx", -1)
    d_pre = d_padded[:, CONV - 1 :].at[:, blk_len - (CONV - 1) :].add(d_edge)
    d_proj = jnp.concatenate(
        [d_pre.reshape(tok_rows, conv_width), d_gate.reshape(tok_rows, VV)], 1
    ).astype(jnp.bfloat16)
    d_rate_rows = d_rate.reshape(tok_rows, 2 * H).astype(jnp.bfloat16)
    d_proj_all, d_rate_all, d_res_all = (
        lax.all_gather(d_proj.reshape(seq_count, blk_len, proj_cols), "ctx", axis=1, tiled=True),
        lax.all_gather(d_rate_rows.reshape(seq_count, blk_len, 2 * H), "ctx", axis=1, tiled=True),
        lax.all_gather(d_res_rows.reshape(seq_count, blk_len, feat_dim), "ctx", axis=1, tiled=True),
    )
    d_proj_all = d_proj_all.reshape(-1, proj_cols)
    d_rate_all = d_rate_all.reshape(-1, 2 * H)
    d_res_all = d_res_all.reshape(-1, feat_dim)
    gated_sub = own_features(gated_all, shard_count, ctx_count, ctx_place).reshape(
        -1, VV // ctx_count
    )
    out_grad = jnp.dot(gated_sub.T, d_res_all, preferred_element_type=jnp.float32)
    proj_grad = jnp.dot(rows_sub.T, d_proj_all, preferred_element_type=jnp.float32)
    rate_grad = jnp.dot(rows_sub.T, d_rate_all, preferred_element_type=jnp.float32)
    normed_share = jnp.dot(d_proj_all, w_proj.T, preferred_element_type=jnp.float32) + jnp.dot(
        d_rate_all, w_rates.T, preferred_element_type=jnp.float32
    )
    normed_share = normed_share.reshape(
        seq_count, -1, shard_count, 1, w_proj.shape[0] // shard_count
    )
    d_normed = (
        lax.all_to_all(
            normed_share.astype(jnp.bfloat16), "ctx", split_axis=1, concat_axis=3, tiled=True
        )
        .astype(normed_share.dtype)
        .reshape(tok_rows, feat_dim)
    )
    d_in_part, gain_one_grad = rms_back(flat_in, scale_in, mixer_gain, d_normed)
    input_grad = d_residual + d_in_part
    proj_shard, rate_shard, out_shard, up_shard, down_shard = (
        lax.psum_scatter(
            proj_grad.astype(jnp.bfloat16), "shard", scatter_dimension=0, tiled=True
        ).astype(jnp.float32),
        lax.psum_scatter(
            rate_grad.astype(jnp.bfloat16), "shard", scatter_dimension=0, tiled=True
        ).astype(jnp.float32),
        lax.psum_scatter(
            out_grad.astype(jnp.bfloat16), "shard", scatter_dimension=0, tiled=True
        ).astype(jnp.float32),
        lax.psum_scatter(
            up_grad.astype(jnp.bfloat16), "shard", scatter_dimension=1, tiled=True
        ).astype(jnp.float32),
        lax.psum_scatter(
            down_grad.astype(jnp.bfloat16), "shard", scatter_dimension=0, tiled=True
        ).astype(jnp.float32),
    )
    small_sums = lax.psum(
        (gain_one_grad, gain_two_grad, kernel_grad, log_grad, bias_grad, gain_out_grad),
        ("shard", "ctx"),
    )
    return (
        block_out.reshape(seq_count, blk_len, feat_dim),
        input_grad.reshape(seq_count, blk_len, feat_dim),
        small_sums[0],
        proj_shard,
        rate_shard,
        small_sums[2],
        small_sums[3],
        small_sums[4],
        small_sums[5],
        out_shard,
        small_sums[1],
        up_shard,
        down_shard,
    )


def solution(mesh):
    return jax.shard_map(
        local,
        mesh=mesh,
        in_specs=(
            P("shard", "ctx", None),
            P(),
            P(("shard", "ctx"), None),
            P(("shard", "ctx"), None),
            P(),
            P(),
            P(),
            P(),
            P(("shard", "ctx"), None),
            P(),
            P(None, ("shard", "ctx"), None),
            P(("shard", "ctx"), None),
            P("shard", "ctx", None),
        ),
        out_specs=(
            P("shard", "ctx", None),
            P("shard", "ctx", None),
            P(),
            P(("shard", "ctx"), None),
            P(("shard", "ctx"), None),
            P(),
            P(),
            P(),
            P(),
            P(("shard", "ctx"), None),
            P(),
            P(None, ("shard", "ctx"), None),
            P(("shard", "ctx"), None),
        ),
        check_vma=False,
    )
```

profile of v0, /device:TPU:0, one launch (start us, length us, event | category | flops | bytes accessed | tf_op | source)
XLA Modules:
  0.0 1555.0 jit_solution(7956506419094219740)
XLA Ops:
  12.1 48.3 %all-gather.20.cloned.1.call-done = bf16[1,1024,1024]{1,2,0:T(8,128)(2,1)} async-done(((bf16[1,256,1024]{1,2,0:T(8,128)(2,1)}), bf16[1,1024,1024]{1,2,0:T(8,128)(2,1)}) %all-gather.20.cloned.1.call-update) | async-done | bytes 2097168 | tf_op jit(solution)/shard_map/all_gather | solution.py:259
  61.6 24.6 %all-gather.22.cloned.1.call-done = bf16[256,3072]{1,0:T(8,128)(2,1)} async-done(((bf16[32,3072]{1,0:T(8,128)(2,1)}), bf16[256,3072]{1,0:T(8,128)(2,1)}) %all-gather.22.cloned.1.call-update) | async-done | bytes 1572880 | tf_op jit(solution)/shard_map/all_gather | solution.py:252
  104.7 201.3 %reduce-scatter.16.cloned.1.call-done = f32[1,256,3072]{2,1,0:T(8,128)} async-done(((f32[1,1024,3072]{2,1,0:T(8,128)}), f32[1,256,3072]{2,1,0:T(8,128)}) %reduce-scatter.16.cloned.1.call-update) | async-done | bytes 3145744 | tf_op jit(solution)/shard_map/reduce_scatter | solution.py:272
  347.8 158.6 %while.123 = (s32[]{:T(128)}, f32[1,4,128,384]{3,2,1,0:T(8,128)S(1)}, f32[4,1,4,64,384]{4,3,2,1,0:T(8,128)}, f32[4,1,4,64,64]{4,3,2,1,0:T(8,128)}, f32[4,1,4,64,...) while((s32[]{:T(128)}, ...), condition=%wide.region_7.8_spmd.clone.clone, body=%wide.region_5.7_spmd.clone.clone.sunk | while | flops 655929856 | bytes 14082509 | solution.py:111
  351.7 21.0 %custom-call.52 = f32[4,1,64,64]{2,3,1,0:T(8,128)} custom-call(f32[4,1,64,64]{3,2,1,0:T(8,128)} %select_bitcast_fusion.4), custom_call_target="InvertDiagBlocksLowerTriangular" | custom-call | tf_op jit(solution)/shard_map/jvp()/while/body/eval_jaxpr/jit(_solve_triangular)/vmap()/triangular_solve | solution.py:85
  391.4 21.0 %custom-call.52 = f32[4,1,64,64]{2,3,1,0:T(8,128)} custom-call(f32[4,1,64,64]{3,2,1,0:T(8,128)} %select_bitcast_fusion.4), custom_call_target="InvertDiagBlocksLowerTriangular" | custom-call | tf_op jit(solution)/shard_map/jvp()/while/body/eval_jaxpr/jit(_solve_triangular)/vmap()/triangular_solve | solution.py:85
  431.0 21.0 %custom-call.52 = f32[4,1,64,64]{2,3,1,0:T(8,128)} custom-call(f32[4,1,64,64]{3,2,1,0:T(8,128)} %select_bitcast_fusion.4), custom_call_target="InvertDiagBlocksLowerTriangular" | custom-call | tf_op jit(solution)/shard_map/jvp()/while/body/eval_jaxpr/jit(_solve_triangular)/vmap()/triangular_solve | solution.py:85
  470.7 21.0 %custom-call.52 = f32[4,1,64,64]{2,3,1,0:T(8,128)} custom-call(f32[4,1,64,64]{3,2,1,0:T(8,128)} %select_bitcast_fusion.4), custom_call_target="InvertDiagBlocksLowerTriangular" | custom-call | tf_op jit(solution)/shard_map/jvp()/while/body/eval_jaxpr/jit(_solve_triangular)/vmap()/triangular_solve | solution.py:85
  515.8 21.1 %all-gather = bf16[4,4,128,128]{3,2,1,0:T(8,128)(2,1)S(1)} all-gather(bf16[1,4,128,128]{3,2,1,0:T(8,128)(2,1)S(1)} %slice.239), channel_id=2, replica_groups=mesh['shard'=8,'ctx'=4] {'ctx'}, dimensions={0}, use_global_device_ids=true | all-gather | bytes 655360 | tf_op jit(solution)/shard_map/all_gather | solution.py:28
  547.5 52.9 %all-gather.24.cloned.1.call-done = bf16[1024,1024]{1,0:T(8,128)(2,1)} async-done(((bf16[32,1024]{1,0:T(8,128)(2,1)}), bf16[1024,1024]{1,0:T(8,128)(2,1)}) %all-gather.24.cloned.1.call-update) | async-done | bytes 2097168 | tf_op jit(solution)/shard_map/all_gather | solution.py:257
  607.3 25.0 %all-gather.26.cloned.1.call-done = bf16[2,704,1024]{2,1,0:T(8,128)(2,1)} async-done(((bf16[2,88,1024]{2,1,0:T(8,128)(2,1)}), bf16[2,704,1024]{2,1,0:T(8,128)(2,1)}) %all-gather.26.cloned.1.call-update) | async-done | bytes 2883600 | tf_op jit(solution)/shard_map/all_gather | solution.py:254
  632.4 47.8 %all-gather.38.cloned.1.call-done = bf16[1024,1024]{1,0:T(8,128)(2,1)} async-done(((bf16[256,1024]{1,0:T(8,128)(2,1)}), bf16[1024,1024]{1,0:T(8,128)(2,1)}) %all-gather.38.cloned.1.call-update) | async-done | bytes 2097168 | tf_op jit(solution)/shard_map/all_gather | solution.py:297
  705.9 47.1 %all-gather.30.cloned.1.call-done = bf16[1,1024,1024]{2,1,0:T(8,128)(2,1)} async-done(((bf16[1,256,1024]{2,1,0:T(8,128)(2,1)}), bf16[1,1024,1024]{2,1,0:T(8,128)(2,1)}) %all-gather.30.cloned.1.call-update) | async-done | bytes 2097168 | tf_op jit(solution)/shard_map/all_gather | solution.py:260
  766.1 42.3 %reduce-scatter.20.cloned.1.call-done = bf16[1,256,1024]{2,1,0:T(8,128)(2,1)} async-done(((bf16[1,1024,1024]{2,1,0:T(8,128)(2,1)}), bf16[1,256,1024]{2,1,0:T(8,128)(2,1)}) %reduce-scatter.20.cloned.1.call-update) | async-done | bytes 524304 | tf_op jit(solution)/shard_map/reduce_scatter | solution.py:310
  831.6 21.2 %all-gather.3 = bf16[4,4,128,128]{3,2,1,0:T(8,128)(2,1)S(1)} all-gather(bf16[1,4,128,128]{3,2,1,0:T(8,128)(2,1)S(1)} %copy.431), channel_id=5, replica_groups=mesh['shard'=8,'ctx'=4] {'ctx'}, dimensions={0}, use_global_device_ids=true | all-gather | bytes 655360 | tf_op jit(solution)/shard_map/all_gather | solution.py:48
  872.1 283.8 %while.124 = (s32[]{:T(128)}, f32[1,4,128,384]{2,3,1,0:T(8,128)S(1)}, f32[4,1,4,64,128]{4,3,0,2,1:T(8,128)}, f32[4,1,4,64,128]{4,3,0,2,1:T(8,128)}, f32[4,1,4,64...) while((s32[]{:T(128)}, ...), condition=%wide.region_29.30_spmd.clone.clone, body=%wide.region_18.29_spmd.clone.clone.sunk | while | flops 1324586240 | bytes 30439196 | solution.py:111
  877.8 19.7 %custom-call.53 = f32[4,1,64,64]{2,3,1,0:T(8,128)S(1)} custom-call(f32[4,1,64,64]{3,2,1,0:T(8,128)S(1)} %select_bitcast_fusion.5), custom_call_target="InvertDiagBlocksLowerTriangular" | custom-call | tf_op jit(solution)/shard_map/transpose(jvp())/while/body/eval_jaxpr/jit(_solve_triangular)/vmap()/triangular_solve | solution.py:85
  1223.5 73.0 %all-gather.32.cloned.1.call-done = bf16[1,1024,3072]{2,1,0:T(8,128)(2,1)} async-done(((bf16[1,256,3072]{2,1,0:T(8,128)(2,1)}), bf16[1,1024,3072]{2,1,0:T(8,128)(2,1)}) %all-gather.32.cloned.1.call-update) | async-done | bytes 6291472 | tf_op jit(solution)/shard_map/all_gather | solution.py:340
  1316.0 19.7 %reduce-scatter.26.cloned.1.call-done = bf16[88,1024]{1,0:T(8,128)(2,1)} async-done(((bf16[704,1024]{1,0:T(8,128)(2,1)}), bf16[88,1024]{1,0:T(8,128)(2,1)}) %reduce-scatter.26.cloned.1.call-update) | async-done | bytes 180240 | tf_op jit(solution)/shard_map/reduce_scatter | solution.py:381
  1337.4 46.3 %reduce-scatter.30.cloned.1.call-done = bf16[88,2048]{1,0:T(8,128)(2,1)} async-done(((bf16[704,2048]{1,0:T(8,128)(2,1)}), bf16[88,2048]{1,0:T(8,128)(2,1)}) %reduce-scatter.30.cloned.1.call-update) | async-done | bytes 360464
  1386.0 34.8 %reduce-scatter.28.cloned.1.call-done = bf16[32,8]{1,0:T(8,128)(2,1)} async-done(((bf16[256,8]{1,0:T(8,128)(2,1)}), bf16[32,8]{1,0:T(8,128)(2,1)}) %reduce-scatter.28.cloned.1.call-update) | async-done | bytes 528
  1422.1 36.4 %reduce-scatter.24.cloned.1.call-done = bf16[32,1024]{1,0:T(8,128)(2,1)} async-done(((bf16[256,1024]{1,0:T(8,128)(2,1)}), bf16[32,1024]{1,0:T(8,128)(2,1)}) %reduce-scatter.24.cloned.1.call-update) | async-done | bytes 65552 | tf_op jit(solution)/shard_map/reduce_scatter | solution.py:375
  1472.1 42.6 %all-reduce.21 = (f32[1024]{0:T(1024)}, f32[4,2048]{1,0:T(4,128)}, f32[4]{0:T(128)}, f32[4]{0:T(128)}, f32[256]{0:T(256)}, /*index=5*/f32[1024]{0:T(1024)}) all-reduce(f32[1024]{0:T(1024)S(1)} %reduce_sum.328, f32[4,2048]{1,0:T(4,128)S(1)} %pad_add_fusion.4, ...), channel_id=1, replica_groups=mesh['shard'=8,'ctx'=4] {'shard','ctx'}, use_global_device_ids=true, to_apply=%region_34.35 | all-reduce | flops 10504 | bytes 84032 | tf_op jit(solution)/shard_map/psum | solution.py:385
  1518.3 27.9 %reduce-scatter.22.cloned.1.call-done = bf16[32,3072]{1,0:T(8,128)(2,1)} async-done(((bf16[256,3072]{1,0:T(8,128)(2,1)}), bf16[32,3072]{1,0:T(8,128)(2,1)}) %reduce-scatter.22.cloned.1.call-update) | async-done | bytes 196624 | tf_op jit(solution)/shard_map/reduce_scatter | solution.py:369
  (697 shorter events, 627.5 us)
Async XLA Ops:
  7.2 53.3 %all-gather.20.cloned.1.call-start = ((), (), s32[]{:S(2)}) async-start(), calls=%async_computation.10 | async-start | bytes 2621440 | tf_op jit(solution)/shard_map/all_gather | solution.py:259
  11.3 74.8 %all-gather.22.cloned.1.call-start = ((), (), s32[]{:S(2)}) async-start(), calls=%async_computation.12 | async-start | bytes 1769472 | tf_op jit(solution)/shard_map/all_gather | solution.py:252
  12.1 293.9 %reduce-scatter.16.cloned.1.call-start = ((), (), s32[]{:S(2)}) async-start(), calls=%async_computation.13 | async-start | bytes 15728640 | tf_op jit(solution)/shard_map/reduce_scatter | solution.py:272
  93.9 235.0 %reduce-scatter.14.cloned.1.call-start = ((), (), s32[]{:S(2)}) async-start(), calls=%async_computation.11 | async-start | bytes 40960 | tf_op jit(solution)/shard_map/reduce_scatter | solution.py:273
  104.6 436.7 %all-gather.36.cloned.1.call-start = ((), (), s32[]{:S(2)}) async-start(), calls=%async_computation.25 | async-start | bytes 1310720 | tf_op jit(solution)/shard_map/all_gather | solution.py:28
  307.8 22.2 %collective-permute-start = (f32[1,3,2048]{2,1,0:T(4,128)S(1)}, f32[1,3,2048]{2,1,0:T(4,128)S(1)}, u32[]{:S(2)}, u32[]{:S(2)}) collective-permute-start(f32[1,3,2048]{2,1,0:T(4,128)S(1)} %slice.158), channel_id=1, source_target_pairs={{0,1},{1,2},{2,3},{4,5},{5,6},{6,7},{8,9},{9,10},{10,11},{12,13},{... | collective-permute-start | bytes 73736 | tf_op jit(solution)/shard_map/ppermute | solution.py:22
  507.2 93.3 %all-gather.24.cloned.1.call-start = ((), (), s32[]{:S(2)}) async-start(), calls=%async_computation.14 | async-start | bytes 2162688 | tf_op jit(solution)/shard_map/all_gather | solution.py:257
  507.8 124.6 %all-gather.26.cloned.1.call-start = ((), (), s32[]{:S(2)}) async-start(), calls=%async_computation.15 | async-start | bytes 3244032 | tf_op jit(solution)/shard_map/all_gather | solution.py:254
  508.6 171.6 %all-gather.38.cloned.1.call-start = ((), (), s32[]{:S(2)}) async-start(), calls=%async_computation.26 | async-start | bytes 2621440 | tf_op jit(solution)/shard_map/all_gather | solution.py:297
  604.4 101.6 %all-gather.28.cloned.1.call-start = ((), (), s32[]{:S(2)}) async-start(), calls=%async_computation.16 | async-start | bytes 1622016 | tf_op jit(solution)/shard_map/all_gather | solution.py:255
  605.1 147.9 %all-gather.30.cloned.1.call-start = ((), (), s32[]{:S(2)}) async-start(), calls=%async_computation.18 | async-start | bytes 2621440 | tf_op jit(solution)/shard_map/all_gather | solution.py:260
  607.3 201.1 %reduce-scatter.20.cloned.1.call-start = ((), (), s32[]{:S(2)}) async-start(), calls=%async_computation.19 | async-start | bytes 2621440 | tf_op jit(solution)/shard_map/reduce_scatter | solution.py:310
  765.8 95.0 %all-gather.40.cloned.1.call-start = ((), (), s32[]{:S(2)}) async-start(), calls=%async_computation.27 | async-start | bytes 1310720 | tf_op jit(solution)/shard_map/all_gather | solution.py:48
  826.4 371.5 %all-gather.34.cloned.1.call-start = ((), (), s32[]{:S(2)}) async-start(), calls=%async_computation.22 | async-start | bytes 2621440 | tf_op jit(solution)/shard_map/all_gather | solution.py:298
  827.1 387.9 %all-gather.42.cloned.1.call-start = ((), (), s32[]{:S(2)}) async-start(), calls=%async_computation.28 | async-start | bytes 2621440 | tf_op jit(solution)/shard_map/all_gather | solution.py:342
  854.7 441.9 %all-gather.32.cloned.1.call-start = ((), (), s32[]{:S(2)}) async-start(), calls=%async_computation.20 | async-start | bytes 7864320 | tf_op jit(solution)/shard_map/all_gather | solution.py:340
  1174.3 5.8 collective-permute-start.1
  1181.7 154.0 %reduce-scatter.26.cloned.1.call-start = ((), (), s32[]{:S(2)}) async-start(), calls=%async_computation.24 | async-start | bytes 1622016 | tf_op jit(solution)/shard_map/reduce_scatter | solution.py:381
  1186.7 197.0 %reduce-scatter.30.cloned.1.call-start = ((), (), s32[]{:S(2)}) async-start(), calls=%async_computation.30 | async-start | bytes 3244032
  1197.8 222.9 %reduce-scatter.28.cloned.1.call-start = ((), (), s32[]{:S(2)}) async-start(), calls=%async_computation.29 | async-start | bytes 73728
  1214.9 243.6 %reduce-scatter.24.cloned.1.call-start = ((), (), s32[]{:S(2)}) async-start(), calls=%async_computation.23 | async-start | bytes 589824 | tf_op jit(solution)/shard_map/reduce_scatter | solution.py:375
  1218.1 296.5 %reduce-scatter.18.cloned.1.call-start = ((), (), s32[]{:S(2)}) async-start(), calls=%async_computation.17 | async-start | bytes 2621440 | tf_op jit(solution)/shard_map/reduce_scatter | solution.py:304
  1223.2 323.0 %reduce-scatter.22.cloned.1.call-start = ((), (), s32[]{:S(2)}) async-start(), calls=%async_computation.21 | async-start | bytes 1769472 | tf_op jit(solution)/shard_map/reduce_scatter | solution.py:369
  1312.1 147.9 %all-to-all-start = ((bf16[4,2,32768]{2,1,0:T(2,128)(2,1)}), bf16[4,2,32768]{2,1,0:T(2,128)(2,1)S(1)}, u32[]{:S(2)}, u32[]{:S(2)}) async-start(bf16[4,2,32768]{2,1,0:T(2,128)(2,1)} %reshape.2160), calls=%async_computation.4 | async-start | bytes 1048576 | tf_op jit(solution)/shard_map/all_to_all | solution.py:360
  (102 other events, 2913.9 us)
Sparse Core Ops, SparseCore 0:
  11.5 48.9 all-gather.19
  62.4 23.7 all-gather.21
  94.1 211.8 reduce-scatter.15
  308.6 20.2 reduce-scatter.13
  507.3 33.9 all-gather.35
  544.1 56.3 all-gather.23
  602.4 29.9 all-gather.25
  634.5 45.6 all-gather.37
  682.1 23.8 all-gather.27
  707.3 45.6 all-gather.29
  766.0 42.4 reduce-scatter.19
  826.5 34.3 all-gather.39
  862.4 46.0 all-gather.33
  909.9 43.8 all-gather.41
  1181.8 114.6 all-gather.31
  1299.7 35.9 reduce-scatter.25
  1339.0 44.7 reduce-scatter.29
  1387.2 33.5 reduce-scatter.27
  1424.4 34.0 reduce-scatter.23
  1460.7 44.5 reduce-scatter.17
  1508.6 37.6 reduce-scatter.21
where the time goes:
time: 1560 us
  waiting for transfers between devices  776 us (50%)
  other arithmetic  274 us (18%)
  matrix products  237 us (15%)
  local copies, waits for them, and re-layouts  133 us (9%)
  blocking collectives  108 us (7%)
  between operations  16.2 us (1%)
    reduce_scatter x1, waiting for transfers between devices, local(): lax.psum_scatter(part_proj, 'ctx', scatter_dimension=1, tiled=True)  201 us
    another operation x24, other arithmetic, block_step(): jax.scipy.linalg.solve_triangular(lower_mat, right_side, lower=True)  170 us
    unnamed x23, waiting for transfers between devices  84.6 us
    all_gather x1, waiting for transfers between devices, local(): lax.all_gather(d_proj.reshape(seq_count, blk_len, proj_cols), 'ctx', axis...  73 us
    all_gather x1, waiting for transfers between devices, local(): w_out = lax.all_gather(mixer_out, ('shard', 'ctx'), axis=0, tiled=True)  52.9 us
    all_gather x1, waiting for transfers between devices, local(): lax.all_gather(normed.reshape(seq_count, blk_len, feat_dim), 'ctx', axis=...  48.3 us
    all_gather x1, waiting for transfers between devices, local(): lax.all_gather(ffn_rows.reshape(seq_count, blk_len, feat_dim), 'ctx', axi...  47.8 us
    all_gather x1, waiting for transfers between devices, local(): lax.all_gather(cot_rows.reshape(seq_count, blk_len, feat_dim), 'ctx', axi...  47.1 us
  transfers between devices with their start and end apart: 24, of which 19 were waited for; matrix products, arithmetic and copies ran while one was open for 27% of the time, Pallas kernels for 0%

commit v1 on v0

v1 whole, which is shorter than its diff:
```python
import functools

import jax
import jax.numpy as jnp
from jax import lax
from jax.experimental import pallas as pl
from jax.experimental.pallas import tpu as pltpu
from jax.sharding import PartitionSpec as P

H = 4
DK = 128
DV = 256
CONV = 4
QK = 512
VV = 1024
LANE = 128

norm_eps = 1e-06
exact_mode = lax.Precision.HIGHEST
F32 = jnp.float32
BF16 = jnp.bfloat16
ALL = ("shard", "ctx")


def dot(a, b, ca=1, cb=0):
    return lax.dot_general(
        a, b, (((ca,), (cb,)), ((), ())), precision=exact_mode, preferred_element_type=F32
    )


def low(a, b, ca=1, cb=0):
    return lax.dot_general(
        a.astype(BF16), b.astype(BF16), (((ca,), (cb,)), ((), ())), preferred_element_type=F32
    )


def column(ref, h):
    x = ref[...]
    lanes = lax.broadcasted_iota(jnp.int32, x.shape, 1)
    return jnp.sum(jnp.where(lanes == h, x, 0.0), 1, keepdims=True)


def unit(raw):
    r = lax.rsqrt(jnp.sum(raw * raw, -1, keepdims=True) + norm_eps)
    return raw * r, r


def iotas(size):
    return (
        lax.broadcasted_iota(jnp.int32, (size, size), 0),
        lax.broadcasted_iota(jnp.int32, (size, size), 1),
    )


def unit_lower_inverse(a):
    size = a.shape[0]
    row, col = iotas(size)
    apart = jnp.bitwise_xor(row, col)
    x = jnp.where(row == col, 1.0, 0.0) - jnp.where(apart == 1, a, 0.0)
    b = 2
    while b < size:
        c = jnp.where((apart >= b) & (apart < 2 * b), a, 0.0)
        x = x - dot(dot(x, c), x)
        b *= 2
    return x


def pair_terms(q, k, gc, gr, beta):
    row, col = iotas(k.shape[0])
    incl = col <= row
    decay = jnp.where(incl, jnp.exp(jnp.where(incl, gc - gr, 0.0)), 0.0)
    kk = dot(k, k, 1, 1)
    qk = dot(q, k, 1, 1)
    below = jnp.where(col < row, decay * kk, 0.0)
    return decay, below, qk * decay, row, col


def core_fwd(q_ref, k_ref, v_ref, g_ref, gr_ref, b_ref, out_ref, map_ref, state_ref, t_ref):
    h = pl.program_id(1)
    q = unit(q_ref[...])[0] * DK ** (-0.5)
    k = unit(k_ref[...])[0]
    gc, gr, beta = column(g_ref, h), gr_ref[...], column(b_ref, h)
    decay, below, p, row, col = pair_terms(q, k, gc, gr, beta)
    t = unit_lower_inverse(beta * below)
    t_ref[...] = t
    growth = jnp.exp(gc)
    size = k.shape[0]
    right = jnp.concatenate([beta * v_ref[...], (beta * growth) * k], 1)
    solved = dot(t, right)
    mixed = dot(p, solved)
    out_ref[...] = mixed[:, :DV]
    map_ref[...] = growth * q - mixed[:, DV:]
    last = gc[size - 1 : size, :]
    state = dot(k * jnp.exp(last - gc), solved, 0, 0)
    r, c = iotas(DK)
    state_ref[:, :DV] = state[:, :DV].astype(BF16)
    state_ref[:, DV:] = (jnp.where(r == c, jnp.exp(last), 0.0) - state[:, DV:]).astype(BF16)


def gate_fwd(place_ref, all_ref, out_ref, map_ref, gate_ref, gain_ref, gated_ref, s0_ref):
    place = place_ref[0]
    devices = all_ref.shape[0]
    s = jnp.zeros((DK, DV), F32)
    for j in range(devices - 1):
        entry = all_ref[j].astype(F32)
        s = jnp.where(j < place, dot(entry[:, DV:], s) + entry[:, :DV], s)
    s0_ref[...] = s
    m = out_ref[...] + dot(map_ref[...], s)
    u = m * lax.rsqrt(jnp.mean(m * m, -1, keepdims=True) + norm_eps)
    g = gate_ref[...]
    gated_ref[...] = (u * gain_ref[...] * (g * jax.nn.sigmoid(g))).astype(BF16)


def gate_bwd(dy_ref, out_ref, map_ref, s0_ref, gate_ref, gain_ref, dm_ref, dg_ref, ds_ref, dgain_ref):
    m = out_ref[...] + dot(map_ref[...], s0_ref[...])
    r = lax.rsqrt(jnp.mean(m * m, -1, keepdims=True) + norm_eps)
    u = m * r
    g, gain, dy = gate_ref[...], gain_ref[...], dy_ref[...]
    sg = jax.nn.sigmoid(g)
    silu = g * sg
    dg_ref[...] = (dy * u * gain * (sg * (1.0 + g * (1.0 - sg)))).astype(BF16)
    dgain_ref[...] = jnp.sum(dy * u * silu, 0, keepdims=True)
    du = dy * gain * silu
    dm = r * (du - u * jnp.mean(du * u, -1, keepdims=True))
    dm_ref[...] = dm
    ds_ref[...] = dot(map_ref[...], dm, 0, 0).astype(BF16)


def core_bwd(
    place_ref, maps_ref, ds_all_ref, q_ref, k_ref, v_ref, g_ref, gr_ref, b_ref, t_ref, s0_ref,
    do_ref, dq_ref, dk_ref, dv_ref, dcol_ref, drow_ref,
):
    h = pl.program_id(1)
    place = place_ref[0]
    devices = maps_ref.shape[0]
    ds = jnp.zeros((DK, DV), F32)
    for j in range(devices - 1, 0, -1):
        new = dot(maps_ref[j].astype(F32), ds, 0, 0) + ds_all_ref[j].astype(F32)
        ds = jnp.where(j > place, new, ds)
    qu, rq = unit(q_ref[...])
    q = qu * DK ** (-0.5)
    k, rk = unit(k_ref[...])
    gc, gr, beta = column(g_ref, h), gr_ref[...], column(b_ref, h)
    decay, below, p, row, col = pair_terms(q, k, gc, gr, beta)
    t, s0, do = t_ref[...], s0_ref[...], do_ref[...]
    growth = jnp.exp(gc)
    size = k.shape[0]
    last = gc[size - 1 : size, :]
    tail = jnp.exp(last - gc)
    kd = k * tail
    seen = dot(k, s0)
    rest = v_ref[...] - growth * seen
    x = dot(t, beta * rest)
    qs = dot(q, s0)
    dx = dot(p, do, 0, 0) + dot(kd, ds)
    dr = dot(t, dx, 0, 0)
    da = jnp.where(col < row, -dot(dr, x, 1, 1), 0.0)
    dp = jnp.where(col <= row, dot(do, x, 1, 1), 0.0)
    dkd = dot(x, ds, 1, 1)
    dv_ref[...] = beta * dr
    dbeta = jnp.sum(dr * rest, 1, keepdims=True) + jnp.sum(da * below, 1, keepdims=True)
    dgrow = jnp.sum(do * qs, 1, keepdims=True) - jnp.sum(beta * dr * seen, 1, keepdims=True)
    dqk = dp * decay
    dkk = da * beta * decay
    dq = dot(growth * do, s0, 1, 1) + dot(dqk, k)
    dk = (
        dot((-beta * growth) * dr, s0, 1, 1)
        + dot(dqk, q, 0, 0)
        + dot(dkk, k)
        + dot(dkk, k, 0, 0)
        + dkd * tail
    )
    dspread = dp * p + da * (beta * below)
    dtail = jnp.sum(dkd * k, 1, keepdims=True) * tail
    dlast = jnp.sum(dtail, 0, keepdims=True) + jnp.exp(last) * jnp.sum(
        jnp.sum(ds * s0, 1, keepdims=True), 0, keepdims=True
    )
    at = lax.broadcasted_iota(jnp.int32, gc.shape, 0)
    dgc = jnp.sum(dspread, 1, keepdims=True) - dtail + dgrow * growth
    dgc = dgc + jnp.where(at == size - 1, dlast, 0.0)
    drow_ref[...] = -jnp.sum(dspread, 0, keepdims=True)
    lane = lax.broadcasted_iota(jnp.int32, dcol_ref.shape, 1)
    dcol_ref[...] = jnp.where(lane == 0, dgc, dbeta)
    du = dq * DK ** (-0.5)
    dq_ref[...] = rq * (du - qu * jnp.sum(du * qu, -1, keepdims=True))
    dk_ref[...] = rk * (dk - k * jnp.sum(dk * k, -1, keepdims=True))


def spec(block, index):
    return pl.BlockSpec(block, index)


def cols(length, width, first=0):
    return spec((None, length, width), lambda b, h: (b, 0, first + h))


def per_head(*block):
    return spec((None, None) + block, lambda b, h: (b, h) + (0,) * len(block))


def gathered(devices, rows, width, at=0):
    return spec((devices, None, None, rows, width), lambda b, h: (0, b, h, 0, at))


def whole(*block):
    return spec((None,) + block, lambda b, h: (b,) + (0,) * len(block))


def call(body, name, seqs, args, in_specs, out_specs, outs, flops):
    size = sum(a.size * a.dtype.itemsize for a in args) + sum(
        o.size * o.dtype.itemsize for o in outs
    )
    return pl.pallas_call(
        body,
        grid=(seqs, H),
        in_specs=in_specs,
        out_specs=out_specs,
        out_shape=outs,
        name=name,
        cost_estimate=pl.CostEstimate(flops=flops, bytes_accessed=size, transcendentals=0),
    )(*args)


def conv_silu(padded, kernel):
    length = padded.shape[1] - (CONV - 1)
    total = kernel[0] * padded[:, 0:length]
    for offset in range(1, CONV):
        total = total + kernel[offset] * padded[:, offset : offset + length]
    return jax.nn.silu(total)


def rates(rate_in, decay_log, decay_bias):
    length = rate_in.shape[1]
    decays = -jnp.exp(decay_log) * jax.nn.softplus(rate_in[..., :H] + decay_bias)
    lower = jnp.tril(jnp.ones((length, length), F32))
    cumul = jnp.einsum("ts,bsh->bth", lower, decays, precision=exact_mode)
    return cumul, jax.nn.sigmoid(rate_in[..., H:])


def shifted(shard, axis, by):
    devices = lax.axis_size(axis)
    pairs = [(i, i + by) for i in range(devices) if 0 <= i + by < devices]
    return lax.ppermute(shard, axis, pairs)


def rms_back(inputs, scale, gain, upstream):
    normal = inputs * scale
    weighted = upstream * gain
    gain_grad = jnp.sum(upstream * normal, axis=0)
    return (scale * (weighted - normal * jnp.mean(weighted * normal, -1, keepdims=True)), gain_grad)


def gather(w):
    return lax.all_gather(w, ALL, axis=0, tiled=True)


def scatter(g):
    return lax.psum_scatter(g.astype(BF16), ALL, scatter_dimension=0, tiled=True).astype(F32)


def mm(a, b):
    return jnp.dot(a, b, preferred_element_type=F32)


def local(
    hidden_in, mixer_gain, mixer_proj, decay_proj, conv_kernel, decay_log, decay_bias,
    output_gain, mixer_out, ffn_gain, ffn_up, ffn_down, cotangent,
):
    seqs, length, feat = hidden_in.shape
    rows = seqs * length
    conv_width = 2 * QK + VV
    proj_cols = conv_width + VV
    rate_cols = 2 * H
    devices = lax.axis_size("ctx")
    place = jnp.reshape(lax.axis_index("ctx"), (1,)).astype(jnp.int32)
    sds = jax.ShapeDtypeStruct

    w_in = gather(
        jnp.concatenate(
            [mixer_proj, decay_proj, jnp.zeros((mixer_proj.shape[0], LANE - rate_cols), BF16)], 1
        )
    )
    w_out = gather(mixer_out)
    up_1, up_2, down = gather(ffn_up[0]), gather(ffn_up[1]), gather(ffn_down)

    flat_in = hidden_in.reshape(rows, feat)
    scale_in = lax.rsqrt(jnp.mean(flat_in * flat_in, -1, keepdims=True) + norm_eps)
    normed = (flat_in * scale_in * mixer_gain).astype(BF16)
    cot_flat = cotangent.reshape(rows, feat)
    cot_rows = cot_flat.astype(BF16)

    projected = mm(normed, w_in).reshape(seqs, length, -1)
    pre_rows = projected[..., :conv_width]
    rate_in = projected[..., proj_cols : proj_cols + rate_cols]
    edge_rows = shifted(pre_rows[:, length - (CONV - 1) :], "ctx", 1)
    padded = jnp.concatenate([edge_rows, pre_rows], 1)
    act, conv_back = jax.vjp(conv_silu, padded, conv_kernel)
    (cumul, beta), rates_back = jax.vjp(rates, rate_in, decay_log, decay_bias)
    cumul_row = jnp.swapaxes(cumul, 1, 2)[:, :, None, :]

    qkv = [cols(length, DK), cols(length, DK, QK // DK), cols(length, DV, 2 * QK // DV)]
    narrow = [whole(length, H), per_head(1, length), whole(length, H)]
    work = seqs * H * length * length * DV
    local_out, query_map, own_state, inverse = call(
        core_fwd, "core_fwd", seqs,
        (act, act, act, cumul, cumul_row, beta),
        qkv + narrow,
        [cols(length, DV), cols(length, DK), per_head(DK, DV + DK), per_head(length, length)],
        [
            sds((seqs, length, VV), F32),
            sds((seqs, length, QK), F32),
            sds((seqs, H, DK, DV + DK), BF16),
            sds((seqs, H, length, length), F32),
        ],
        200 * work,
    )
    states = lax.all_gather(own_state, "ctx")
    gain_row = output_gain.reshape(1, DV)
    gain_spec = spec((1, DV), lambda b, h: (0, 0))
    place_spec = pl.BlockSpec(memory_space=pltpu.SMEM)
    gate_spec = cols(length, DV, conv_width // DV)
    gated, state_in = call(
        gate_fwd, "gate_fwd", seqs,
        (place, states, local_out, query_map, projected, gain_row),
        [place_spec, gathered(devices, DK, DV + DK), cols(length, DV), cols(length, DK),
         gate_spec, gain_spec],
        [cols(length, DV), per_head(DK, DV)],
        [sds((seqs, length, VV), BF16), sds((seqs, H, DK, DV), F32)],
        20 * work,
    )
    gated_rows = gated.reshape(rows, VV)
    residual = flat_in + mm(gated_rows, w_out)
    scale_mid = lax.rsqrt(jnp.mean(residual * residual, -1, keepdims=True) + norm_eps)
    ffn_rows = (residual * scale_mid * ffn_gain).astype(BF16)

    up_one, up_two = mm(ffn_rows, up_1.T), mm(ffn_rows, up_2.T)
    sigma = jax.nn.sigmoid(up_one)
    activ = (up_one * sigma * up_two).astype(BF16)
    block_out = residual + mm(activ, down)
    d_activ = mm(cot_rows, down.T)
    d_one = (d_activ * up_two * sigma * (1.0 + up_one * (1.0 - sigma))).astype(BF16)
    d_two = (d_activ * up_one * sigma).astype(BF16)
    down_shard = scatter(mm(activ.T, cot_rows))
    up_shard = jnp.stack([scatter(mm(d_one.T, ffn_rows)), scatter(mm(d_two.T, ffn_rows))])
    d_ffn = mm(d_one, up_1) + mm(d_two, up_2)

    d_res_part, gain_two_grad = rms_back(residual, scale_mid, ffn_gain, d_ffn)
    d_residual = cot_flat + d_res_part
    d_res_rows = d_residual.astype(BF16)
    out_shard = scatter(mm(gated_rows.T, d_res_rows))
    d_gated = mm(d_res_rows, w_out.T).reshape(seqs, length, VV)
    d_mixed, d_gate, own_ds, gain_out_part = call(
        gate_bwd, "gate_bwd", seqs,
        (d_gated, local_out, query_map, state_in, projected, gain_row),
        [cols(length, DV), cols(length, DV), cols(length, DK), per_head(DK, DV), gate_spec,
         gain_spec],
        [cols(length, DV), cols(length, DV), per_head(DK, DV), per_head(1, DV)],
        [
            sds((seqs, length, VV), F32),
            sds((seqs, length, VV), BF16),
            sds((seqs, H, DK, DV), BF16),
            sds((seqs, H, 1, DV), F32),
        ],
        20 * work,
    )
    d_states = lax.all_gather(own_ds, "ctx")
    d_q, d_k, d_v, d_cols, d_rows = call(
        core_bwd, "core_bwd", seqs,
        (place, states, d_states, act, act, act, cumul, cumul_row, beta, inverse, state_in, d_mixed),
        [place_spec, gathered(devices, DK, DK, DV // DK), gathered(devices, DK, DV)]
        + qkv + narrow
        + [per_head(length, length), per_head(DK, DV), cols(length, DV)],
        [cols(length, DK), cols(length, DK), cols(length, DV), per_head(length, 2),
         per_head(1, length)],
        [
            sds((seqs, length, QK), F32),
            sds((seqs, length, QK), F32),
            sds((seqs, length, VV), F32),
            sds((seqs, H, length, 2), F32),
            sds((seqs, H, 1, length), F32),
        ],
        120 * work,
    )
    d_padded, kernel_grad = conv_back(jnp.concatenate([d_q, d_k, d_v], -1))
    d_cumul = jnp.swapaxes(d_cols[..., 0] + d_rows[:, :, 0], 1, 2)
    d_beta = jnp.swapaxes(d_cols[..., 1], 1, 2)
    d_rate, log_grad, bias_grad = rates_back((d_cumul, d_beta))
    d_edge = shifted(d_padded[:, : CONV - 1], "ctx", -1)
    d_pre = d_padded[:, CONV - 1 :].at[:, length - (CONV - 1) :].add(d_edge)
    d_proj = jnp.concatenate(
        [
            d_pre.reshape(rows, conv_width).astype(BF16),
            d_gate.reshape(rows, VV),
            d_rate.reshape(rows, rate_cols).astype(BF16),
            jnp.zeros((rows, LANE - rate_cols), BF16),
        ],
        1,
    )
    in_shard = scatter(mm(normed.T, d_proj))
    d_normed = mm(d_proj, w_in.T)
    d_in_part, gain_one_grad = rms_back(flat_in, scale_in, mixer_gain, d_normed)
    input_grad = d_residual + d_in_part

    small = (
        gain_one_grad, gain_two_grad, kernel_grad, log_grad, bias_grad,
        jnp.sum(gain_out_part, (0, 1, 2)),
    )
    flat = jnp.concatenate([s.reshape(-1) for s in small])
    pad = -flat.shape[0] % (8 * LANE)
    total = lax.psum(jnp.pad(flat, (0, pad)).reshape(-1, LANE), ALL).reshape(-1)
    sums, start = [], 0
    for s in small:
        sums.append(total[start : start + s.size].reshape(s.shape))
        start += s.size
    return (
        block_out.reshape(seqs, length, feat),
        input_grad.reshape(seqs, length, feat),
        sums[0],
        in_shard[:, :proj_cols],
        in_shard[:, proj_cols : proj_cols + rate_cols],
        sums[2],
        sums[3],
        sums[4],
        sums[5],
        out_shard,
        sums[1],
        up_shard,
        down_shard,
    )


def solution(mesh):
    split = P(ALL, None)
    block = P("shard", "ctx", None)
    up = P(None, ALL, None)
    return jax.shard_map(
        local,
        mesh=mesh,
        in_specs=(block, P(), split, split, P(), P(), P(), P(), split, P(), up, split, block),
        out_specs=(block, block, P(), split, split, P(), P(), P(), P(), split, P(), up, split),
        check_vma=False,
    )
```

time: 1560 us -> 1240 us (0.79)
  other arithmetic: 274 us -> 25.4 us
  waiting for transfers between devices: 776 us -> 970 us
  matrix products: 237 us -> 68.1 us
  local copies, waits for them, and re-layouts: 133 us -> 29.7 us
  Pallas kernels: 0 us -> 74.3 us
  blocking collectives: 108 us -> 40.5 us
    reduce_scatter x7 -> x5, waiting for transfers between devices: 345 us -> 667 us  [scatter(): lax.psum_scatter(g.astype(BF16), ALL, scatter_dimension=0, tiled=True)]
    another operation x56 -> x1, other arithmetic: 183 us -> 1.91 us  [local(): jnp.stack([scatter(mm(d_one.T, ffn_rows)), scatter(mm(d_two.T, ffn_rows))])]
    dot_general x102 -> x17, matrix products: 214 us -> 68.1 us  [the longest x15 66.7 us: mm(): return jnp.dot(a, b, preferred_element_type=F32)]
    unnamed x23 -> x12, waiting for transfers between devices: 84.6 us -> 1.89 us
    pallas_call x0 -> x4, Pallas kernels: none -> 74.3 us  [call(): pl.pallas_call(body, grid=(seqs, H), in_specs=in_specs, out_specs=out_spe...]
    all_gather x4 -> x0, blocking collectives: 65.5 us -> none  [the longest x1 21.2 us: carried_in_2(): lax.all_gather(part.astype(kind), axis)]
    all_gather x12 -> x7, waiting for transfers between devices: 343 us -> 299 us  [the longest x5 261 us: gather(): return lax.all_gather(w, ALL, axis=0, tiled=True)]
    reduce_sum x27 -> x1, other arithmetic: 34.4 us -> 1.42 us  [local(): jnp.sum(gain_out_part, (0, 1, 2))]
  transfers between devices with their start and end apart: 24 -> 14, of which waited for: 19 -> 13; matrix products, arithmetic and copies ran while one was open for 27% -> 8% of each run, Pallas kernels for 0% -> 6%
where the time goes in v1:
time: 1240 us; the launch traced here: 1230 us
  waiting for transfers between devices  970 us (78%)
  Pallas kernels  74.3 us (6%)
  matrix products  68.1 us (5%)
  blocking collectives  40.5 us (3%)
  local copies, waits for them, and re-layouts  29.7 us (2%)
  other arithmetic  25.4 us (2%)
  between operations  15.2 us (1%)
    reduce_scatter x5, waiting for transfers between devices, scatter(): lax.psum_scatter(g.astype(BF16), ALL, scatter_dimension=0, tiled=True)  667 us
    all_gather x5, waiting for transfers between devices, gather(): return lax.all_gather(w, ALL, axis=0, tiled=True)  261 us
    pallas_call x4, Pallas kernels, call(): pl.pallas_call(body, grid=(seqs, H), in_specs=in_specs, out_specs=out_spe...  74.3 us
    dot_general x15, matrix products, mm(): return jnp.dot(a, b, preferred_element_type=F32)  66.7 us
    psum x1, blocking collectives, local(): total = lax.psum(jnp.pad(flat, (0, pad)).reshape(-1, LANE), ALL).reshape(-1)  40.5 us
    all_gather x1, waiting for transfers between devices, local(): states = lax.all_gather(own_state, 'ctx')  31.9 us
  transfers between devices with their start and end apart: 14, of which 13 were waited for; matrix products, arithmetic and copies ran while one was open for 8% of the time, Pallas kernels for 6%

profile of v1, /device:TPU:0, one launch (start us, length us, event | category | flops | bytes accessed | tf_op | source)
XLA Modules:
  0.0 1229.0 jit_solution(5725682717112792895)
XLA Ops:
  13.5 71.0 %all-gather.12.cloned.1.call-done = bf16[1024,3200]{1,0:T(8,128)(2,1)} async-done(((bf16[32,3200]{1,0:T(8,128)(2,1)}), bf16[1024,3200]{1,0:T(8,128)(2,1)}) %all-gather.12.cloned.1.call-update) | async-done | bytes 6553616 | tf_op jit(solution)/shard_map/all_gather | solution.py:254
  84.5 5.2 convolution_bitcast_fusion.gate_ref
  97.3 6.1 fusion.12
  103.4 36.3 %core_fwd.1 = (f32[1,256,1024]{2,1,0:T(8,128)}, f32[1,256,512]{2,1,0:T(8,128)}, bf16[1,4,128,384]{3,2,1,0:T(8,128)(2,1)}, f32[1,4,256,256]{3,2,1,0:T(8,128)}) custom-call(f32[1,256,2048]{2,1,0:T(8,128)} %get-tuple-element.105.q_ref.k_ref.v_ref, f32[1,256,2048]{2,1,0:T(8,128)} %get-tuple-element.105.q_ref.k_ref.v_ref, ...), custom_call_target="tpu_custom_call" | custom-call | flops 13421772800 | bytes 9318400 | tf_op jit(solution)/shard_map/core_fwd/pallas_call | solution.py:213
  142.0 11.2 all-gather.16.cloned.1.call-done
  153.2 6.0 fusion.58
  159.1 31.9 %all-gather.18.cloned.1.call-done = bf16[4,4,128,384]{3,2,1,0:T(8,128)(2,1)} async-done(((bf16[1,4,128,384]{3,2,1,0:T(8,128)(2,1)}), bf16[4,4,128,384]{3,2,1,0:T(8,128)(2,1)}) %all-gather.18.cloned.1.call-update) | async-done | bytes 1572880 | tf_op jit(solution)/shard_map/all_gather | solution.py:317
  191.1 7.5 gate_fwd.1
  198.6 50.5 %all-gather.14.cloned.1.call-done = bf16[1024,1024]{1,0:T(8,128)(2,1)} async-done(((bf16[32,1024]{1,0:T(8,128)(2,1)}), bf16[1024,1024]{1,0:T(8,128)(2,1)}) %all-gather.14.cloned.1.call-update) | async-done | bytes 2097168 | tf_op jit(solution)/shard_map/all_gather | solution.py:254
  252.9 65.1 %all-gather.22.cloned.1.call-done = bf16[1,2816,1024]{2,1,0:T(8,128)(2,1)} async-done(((bf16[1,88,1024]{2,1,0:T(8,128)(2,1)}), bf16[1,2816,1024]{2,1,0:T(8,128)(2,1)}) %all-gather.22.cloned.1.call-update) | async-done | bytes 5767184 | tf_op jit(solution)/shard_map/all_gather | solution.py:254
  318.0 6.2 fusion.2
  324.2 63.0 %all-gather.20.cloned.1.call-done = bf16[1,2816,1024]{2,1,0:T(8,128)(2,1)} async-done(((bf16[1,88,1024]{2,1,0:T(8,128)(2,1)}), bf16[1,2816,1024]{2,1,0:T(8,128)(2,1)}) %all-gather.20.cloned.1.call-update) | async-done | bytes 5767184 | tf_op jit(solution)/shard_map/all_gather | solution.py:254
  387.3 8.6 multiply_convert_fusion.1
  405.6 6.2 gate_bwd.1
  415.3 5.5 fusion.60
  432.2 6.4 all-gather.24.cloned.1.call-done
  438.6 24.4 %core_bwd.1 = (f32[1,256,512]{2,1,0:T(8,128)}, f32[1,256,512]{2,1,0:T(8,128)}, f32[1,256,1024]{2,1,0:T(8,128)}, f32[1,4,256,2]{3,2,1,0:T(8,128)}, f32[1,4,1,256]{3,2,1,0:T(1,128)}) custom-call(s32[1]{0:T(128)} %bitcast.1.place_ref, bf16[4,1,4,128,384]{4,3,2,1,0:T(8,128)(2,1)} %bitcast.150, bf16[4,1,4,128,256]{4,3,2,1,0:T(8,128)(2,1)} %bitcast.173, ...), custom_call_target="tpu_custom_call" | custom-call | flops 8053063680 | bytes 13656068 | tf_op jit(solution)/shard_map/core_bwd/pallas_call | solution.py:213
  491.8 5.4 fusion.16
  502.5 40.5 %psum.7 = f32[88,128]{1,0:T(8,128)S(1)} all-reduce(f32[88,128]{1,0:T(8,128)S(1)} %pad_bitcast_fusion), channel_id=1, replica_groups=mesh['shard'=8,'ctx'=4] {'shard','ctx'}, use_global_device_ids=true, to_apply=%region_13.14 | all-reduce | flops 11264 | bytes 90112 | tf_op jit(solution)/shard_map/psum | solution.py:410
  546.7 33.6 %reduce-scatter.8.cloned.1.call-done = bf16[32,1024]{1,0:T(8,128)(2,1)} async-done(((bf16[1024,1024]{1,0:T(8,128)(2,1)}), bf16[32,1024]{1,0:T(8,128)(2,1)}) %reduce-scatter.8.cloned.1.call-update) | async-done | bytes 65552 | tf_op jit(solution)/shard_map/reduce_scatter | solution.py:258
  581.8 156.8 %reduce-scatter.14.cloned.1.call-done = bf16[88,1024]{1,0:T(8,128)(2,1)} async-done(((bf16[2816,1024]{1,0:T(8,128)(2,1)}), bf16[88,1024]{1,0:T(8,128)(2,1)}) %reduce-scatter.14.cloned.1.call-update) | async-done | bytes 180240 | tf_op jit(solution)/shard_map/reduce_scatter | solution.py:258
  740.3 157.5 %reduce-scatter.12.cloned.1.call-done = bf16[88,1024]{1,0:T(8,128)(2,1)} async-done(((bf16[2816,1024]{1,0:T(8,128)(2,1)}), bf16[88,1024]{1,0:T(8,128)(2,1)}) %reduce-scatter.12.cloned.1.call-update) | async-done | bytes 180240 | tf_op jit(solution)/shard_map/reduce_scatter | solution.py:258
  897.9 159.0 %reduce-scatter.10.cloned.1.call-done = bf16[88,1024]{1,0:T(8,128)(2,1)} async-done(((bf16[2816,1024]{1,0:T(8,128)(2,1)}), bf16[88,1024]{1,0:T(8,128)(2,1)}) %reduce-scatter.10.cloned.1.call-update) | async-done | bytes 180240 | tf_op jit(solution)/shard_map/reduce_scatter | solution.py:258
  1058.7 159.9 %reduce-scatter.6.cloned.1.call-done = bf16[32,3200]{1,0:T(8,128)(2,1)} async-done(((bf16[1024,3200]{1,0:T(8,128)(2,1)}), bf16[32,3200]{1,0:T(8,128)(2,1)}) %reduce-scatter.6.cloned.1.call-update) | async-done | bytes 204816 | tf_op jit(solution)/shard_map/reduce_scatter | solution.py:258
  (160 shorter events, 90.0 us)
Async XLA Ops:
  7.2 77.3 %all-gather.12.cloned.1.call-start = ((), (), s32[]{:S(2)}) async-start(), calls=%async_computation.5 | async-start | bytes 6758400 | tf_op jit(solution)/shard_map/all_gather | solution.py:254
  9.7 143.4 %all-gather.16.cloned.1.call-start = ((), (), s32[]{:S(2)}) async-start(), calls=%async_computation.7 | async-start | bytes 5947392 | tf_op jit(solution)/shard_map/all_gather | solution.py:254
  10.5 180.6 %all-gather.18.cloned.1.call-start = ((), (), s32[]{:S(2)}) async-start(), calls=%async_computation.13 | async-start | bytes 1966080 | tf_op jit(solution)/shard_map/all_gather | solution.py:317
  13.5 80.4 %copy-start.31 = (f32[4]{0:T(128)S(1)}, f32[4]{0:T(128)}, u32[]{:S(2)}) copy-start(f32[4]{0:T(128)} %param.21) | copy-start | bytes 52
  89.7 6.2 copy-start
  89.7 7.6 collective-permute-start
  103.4 37.0 %copy-start.20 = (bf16[2,88,1024]{2,1,0:T(8,128)(2,1)S(1)}, bf16[2,88,1024]{2,1,0:T(8,128)(2,1)}, u32[]{:S(2)}) copy-start(bf16[2,88,1024]{2,1,0:T(8,128)(2,1)} %param.25) | copy-start | bytes 1081348
  103.4 49.8 %copy-start.6 = (f32[1,256,1024]{2,1,0:T(8,128)S(1)}, f32[1,256,1024]{2,1,0:T(8,128)}, u32[]{:S(2)}) copy-start(f32[1,256,1024]{2,1,0:T(8,128)} %param.27) | copy-start | bytes 3145732
  139.7 109.4 %all-gather.14.cloned.1.call-start = ((), (), s32[]{:S(2)}) async-start(), calls=%async_computation.6 | async-start | bytes 2162688 | tf_op jit(solution)/shard_map/all_gather | solution.py:254
  140.3 177.7 %all-gather.22.cloned.1.call-start = ((), (), s32[]{:S(2)}) async-start(), calls=%async_computation.15 | async-start | bytes 5947392 | tf_op jit(solution)/shard_map/all_gather | solution.py:254
  141.2 246.1 %all-gather.20.cloned.1.call-start = ((), (), s32[]{:S(2)}) async-start(), calls=%async_computation.14 | async-start | bytes 5947392 | tf_op jit(solution)/shard_map/all_gather | solution.py:254
  141.7 296.8 %all-gather.24.cloned.1.call-start = ((), (), s32[]{:S(2)}) async-start(), calls=%async_computation.16 | async-start | bytes 1310720 | tf_op jit(solution)/shard_map/all_gather | solution.py:366
  191.1 58.0 %copy-start.2 = (f32[1,256,1024]{2,1,0:T(8,128)S(1)}, f32[1,256,1024]{2,1,0:T(8,128)}, u32[]{:S(2)}) copy-start(f32[1,256,1024]{2,1,0:T(8,128)} %param.15) | copy-start | bytes 3145732
  251.7 145.9 %copy-start.7 = (f32[256,1024]{1,0:T(8,128)}, f32[256,1024]{1,0:T(8,128)S(1)}, u32[]{:S(2)}) copy-start(f32[256,1024]{1,0:T(8,128)S(1)} %get-tuple-element.127) | copy-start | bytes 3145732
  387.2 8.6 copy-start.29
  403.9 8.2 copy-start.4
  411.8 168.5 %reduce-scatter.8.cloned.1.call-start = ((), (), s32[]{:S(2)}) async-start(), calls=%async_computation.9 | async-start | bytes 2162688 | tf_op jit(solution)/shard_map/reduce_scatter | solution.py:258
  415.2 323.4 %reduce-scatter.14.cloned.1.call-start = ((), (), s32[]{:S(2)}) async-start(), calls=%async_computation.12 | async-start | bytes 5947392 | tf_op jit(solution)/shard_map/reduce_scatter | solution.py:258
  420.8 477.0 %reduce-scatter.12.cloned.1.call-start = ((), (), s32[]{:S(2)}) async-start(), calls=%async_computation.11 | async-start | bytes 5947392 | tf_op jit(solution)/shard_map/reduce_scatter | solution.py:258
  426.6 630.2 %reduce-scatter.10.cloned.1.call-start = ((), (), s32[]{:S(2)}) async-start(), calls=%async_computation.10 | async-start | bytes 5947392 | tf_op jit(solution)/shard_map/reduce_scatter | solution.py:258
  432.1 786.6 %reduce-scatter.6.cloned.1.call-start = ((), (), s32[]{:S(2)}) async-start(), calls=%async_computation.8 | async-start | bytes 6758400 | tf_op jit(solution)/shard_map/reduce_scatter | solution.py:258
  462.9 7.9 copy-start.3
  475.6 6.1 collective-permute-start.1
  497.3 48.2 %copy-start.5 = (f32[256,1024]{1,0:T(8,128)S(1)}, f32[256,1024]{1,0:T(8,128)}, u32[]{:S(2)}) copy-start(f32[256,1024]{1,0:T(8,128)} %copy-done.4) | copy-start | bytes 3145732
  (25 other events, 84.8 us)
Sparse Core Ops, SparseCore 0:
  11.4 73.0 all-gather.11
  87.3 65.8 all-gather.15
  155.3 35.7 all-gather.17
  193.9 55.2 all-gather.13
  251.8 66.1 all-gather.21
  321.3 65.9 all-gather.19
  411.9 26.6 all-gather.23
  440.8 139.4 reduce-scatter.7
  582.6 156.0 reduce-scatter.13
  740.8 157.0 reduce-scatter.11
  900.2 156.6 reduce-scatter.9
  1059.0 159.6 reduce-scatter.5

commit v2 on v1

--- a/solution.py
+++ b/solution.py
@@ -254,8 +254,27 @@
     return lax.all_gather(w, ALL, axis=0, tiled=True)
 
 
-def scatter(g):
-    return lax.psum_scatter(g.astype(BF16), ALL, scatter_dimension=0, tiled=True).astype(F32)
+def gather_all(parts):
+    width = parts[0].shape[1]
+    shares = gather(jnp.concatenate(parts, 0)).reshape(-1, sum(p.shape[0] for p in parts), width)
+    found, start = [], 0
+    for p in parts:
+        found.append(shares[:, start : start + p.shape[0]].reshape(-1, width))
+        start += p.shape[0]
+    return found
+
+
+def scatter_all(grads, devices):
+    shares = [g.astype(BF16).reshape(devices, -1, g.shape[1]) for g in grads]
+    sent = jnp.concatenate(shares, 1)
+    own = lax.psum_scatter(
+        sent.reshape(-1, sent.shape[2]), ALL, scatter_dimension=0, tiled=True
+    ).astype(F32)
+    found, start = [], 0
+    for p in shares:
+        found.append(own[start : start + p.shape[1]])
+        start += p.shape[1]
+    return found
 
 
 def mm(a, b):
@@ -280,8 +299,7 @@
             [mixer_proj, decay_proj, jnp.zeros((mixer_proj.shape[0], LANE - rate_cols), BF16)], 1
         )
     )
-    w_out = gather(mixer_out)
-    up_1, up_2, down = gather(ffn_up[0]), gather(ffn_up[1]), gather(ffn_down)
+    w_out, up_1, up_2, down = gather_all((mixer_out, ffn_up[0], ffn_up[1], ffn_down))
 
     flat_in = hidden_in.reshape(rows, feat)
     scale_in = lax.rsqrt(jnp.mean(flat_in * flat_in, -1, keepdims=True) + norm_eps)
@@ -340,14 +358,14 @@
     d_activ = mm(cot_rows, down.T)
     d_one = (d_activ * up_two * sigma * (1.0 + up_one * (1.0 - sigma))).astype(BF16)
     d_two = (d_activ * up_one * sigma).astype(BF16)
-    down_shard = scatter(mm(activ.T, cot_rows))
-    up_shard = jnp.stack([scatter(mm(d_one.T, ffn_rows)), scatter(mm(d_two.T, ffn_rows))])
+    down_grad = mm(activ.T, cot_rows).astype(BF16)
+    up_grads = [mm(d_one.T, ffn_rows).astype(BF16), mm(d_two.T, ffn_rows).astype(BF16)]
     d_ffn = mm(d_one, up_1) + mm(d_two, up_2)
 
     d_res_part, gain_two_grad = rms_back(residual, scale_mid, ffn_gain, d_ffn)
     d_residual = cot_flat + d_res_part
     d_res_rows = d_residual.astype(BF16)
-    out_shard = scatter(mm(gated_rows.T, d_res_rows))
+    out_grad = mm(gated_rows.T, d_res_rows).astype(BF16)
     d_gated = mm(d_res_rows, w_out.T).reshape(seqs, length, VV)
     d_mixed, d_gate, own_ds, gain_out_part = call(
         gate_bwd, "gate_bwd", seqs,
@@ -396,14 +414,20 @@
         ],
         1,
     )
-    in_shard = scatter(mm(normed.T, d_proj))
+    in_grad = mm(normed.T, d_proj)
+    parts = [in_grad[:, at : at + feat] for at in range(0, proj_cols, feat)]
+    rate_grad = in_grad[:, proj_cols : proj_cols + rate_cols]
+    down_shard, up_s1, up_s2, out_shard, *in_shards = scatter_all(
+        [down_grad] + up_grads + [out_grad] + parts, devices * lax.axis_size("shard")
+    )
+    up_shard = jnp.stack([up_s1, up_s2])
     d_normed = mm(d_proj, w_in.T)
     d_in_part, gain_one_grad = rms_back(flat_in, scale_in, mixer_gain, d_normed)
     input_grad = d_residual + d_in_part
 
     small = (
         gain_one_grad, gain_two_grad, kernel_grad, log_grad, bias_grad,
-        jnp.sum(gain_out_part, (0, 1, 2)),
+        jnp.sum(gain_out_part, (0, 1, 2)), rate_grad,
     )
     flat = jnp.concatenate([s.reshape(-1) for s in small])
     pad = -flat.shape[0] % (8 * LANE)
@@ -412,12 +436,15 @@
     for s in small:
         sums.append(total[start : start + s.size].reshape(s.shape))
         start += s.size
+    own_rows = decay_proj.shape[0]
+    me = lax.axis_index("shard") * devices + lax.axis_index("ctx")
+    rate_shard = lax.dynamic_slice_in_dim(sums[6], me * own_rows, own_rows, 0)
     return (
         block_out.reshape(seqs, length, feat),
         input_grad.reshape(seqs, length, feat),
         sums[0],
-        in_shard[:, :proj_cols],
-        in_shard[:, proj_cols : proj_cols + rate_cols],
+        jnp.concatenate(in_shards, 1),
+        rate_shard,
         sums[2],
         sums[3],
         sums[4],

time: 1240 us -> 1130 us (0.911)
  waiting for transfers between devices: 970 us -> 881 us
  blocking collectives: 40.5 us -> 0 us
  local copies, waits for them, and re-layouts: 29.7 us -> 65.8 us
  matrix products: 68.1 us -> 49.9 us
    reduce_scatter x5 -> x1, waiting for transfers between devices: 667 us -> 549 us  [scatter_all(): lax.psum_scatter(sent.reshape(-1, sent.shape[2]), ALL, scatter_dimension=...]
    psum x0 -> x1, waiting for transfers between devices: none -> 104 us  [local(): total = lax.psum(jnp.pad(flat, (0, pad)).reshape(-1, LANE), ALL).reshape(-1)]
    all_gather x5 -> x2, waiting for transfers between devices: 261 us -> 193 us  [gather(): return lax.all_gather(w, ALL, axis=0, tiled=True)]
    psum x1 -> x0, blocking collectives: 40.5 us -> none  [local(): total = lax.psum(jnp.pad(flat, (0, pad)).reshape(-1, LANE), ALL).reshape(-1)]
    dot_general x15, matrix products: 66.7 us -> 47.9 us  [mm(): return jnp.dot(a, b, preferred_element_type=F32)]
    unnamed x75 -> x85, local copies, waits for them, and re-layouts: 10.1 us -> 26.4 us
  transfers between devices with their start and end apart: 14 -> 8, of which waited for: 13 -> 7; matrix products, arithmetic and copies ran while one was open for 8% -> 5% of each run, Pallas kernels for 6% -> 1%
where the time goes in v2:
time: 1130 us; the launch traced here: 1120 us
  waiting for transfers between devices  881 us (78%)
  Pallas kernels  74.4 us (7%)
  local copies, waits for them, and re-layouts  65.8 us (6%)
  matrix products  49.9 us (4%)
  other arithmetic  27.8 us (2%)
  between operations  15 us (1%)
    reduce_scatter x1, waiting for transfers between devices, scatter_all(): lax.psum_scatter(sent.reshape(-1, sent.shape[2]), ALL, scatter_dimension=...  549 us
    all_gather x2, waiting for transfers between devices, gather(): return lax.all_gather(w, ALL, axis=0, tiled=True)  193 us
    psum x1, waiting for transfers between devices, local(): total = lax.psum(jnp.pad(flat, (0, pad)).reshape(-1, LANE), ALL).reshape(-1)  104 us
    pallas_call x4, Pallas kernels, call(): pl.pallas_call(body, grid=(seqs, H), in_specs=in_specs, out_specs=out_spe...  74.4 us
    dot_general x15, matrix products, mm(): return jnp.dot(a, b, preferred_element_type=F32)  47.9 us
    all_gather x1, waiting for transfers between devices, local(): states = lax.all_gather(own_state, 'ctx')  33.5 us
    unnamed x85, local copies, waits for them, and re-layouts  26.4 us
  transfers between devices with their start and end apart: 8, of which 7 were waited for; matrix products, arithmetic and copies ran while one was open for 5% of the time, Pallas kernels for 1%

profile of v2, /device:TPU:0, one launch (start us, length us, event | category | flops | bytes accessed | tf_op | source)
XLA Modules:
  0.0 1119.8 jit_solution(1767115864953513329)
XLA Ops:
  12.8 71.7 %all-gather.7.cloned.1.call-done = bf16[1024,3200]{1,0:T(8,128)(2,1)} async-done(((bf16[32,3200]{1,0:T(8,128)(2,1)}), bf16[1024,3200]{1,0:T(8,128)(2,1)}) %all-gather.7.cloned.1.call-update) | async-done | bytes 6553616 | tf_op jit(solution)/shard_map/all_gather | solution.py:254
  84.5 5.2 convolution_bitcast_fusion.gate_ref
  90.6 3.4 collective-permute-start
  97.5 6.4 fusion.4
  103.9 36.3 %core_fwd.1 = (f32[1,256,1024]{2,1,0:T(8,128)}, f32[1,256,512]{2,1,0:T(8,128)}, bf16[1,4,128,384]{3,2,1,0:T(8,128)(2,1)}, f32[1,4,256,256]{3,2,1,0:T(8,128)}) custom-call(f32[1,256,2048]{2,1,0:T(8,128)} %get-tuple-element.105.q_ref.k_ref.v_ref, f32[1,256,2048]{2,1,0:T(8,128)} %get-tuple-element.105.q_ref.k_ref.v_ref, ...), custom_call_target="tpu_custom_call" | custom-call | flops 13421772800 | bytes 9318400 | tf_op jit(solution)/shard_map/core_fwd/pallas_call | solution.py:213
  141.5 33.5 %all-gather.11.cloned.1.call-done = bf16[4,4,128,384]{3,2,1,0:T(8,128)(2,1)} async-done(((bf16[1,4,128,384]{3,2,1,0:T(8,128)(2,1)}), bf16[4,4,128,384]{3,2,1,0:T(8,128)(2,1)}) %all-gather.11.cloned.1.call-update) | async-done | bytes 1572880 | tf_op jit(solution)/shard_map/all_gather | solution.py:335
  174.9 7.4 gate_fwd.1
  182.4 121.2 %all-gather.9.cloned.1.call-done = bf16[9472,1024]{1,0:T(8,128)(2,1)} async-done(((bf16[296,1024]{1,0:T(8,128)(2,1)}), bf16[9472,1024]{1,0:T(8,128)(2,1)}) %all-gather.9.cloned.1.call-update) | async-done | bytes 19398672 | tf_op jit(solution)/shard_map/all_gather | solution.py:254
  305.4 7.4 fusion.45
  317.3 4.3 multiply_convert_fusion
  323.3 4.1 convolution_convert_fusion.1
  332.0 6.2 gate_bwd.1
  338.7 5.6 fusion.51
  344.8 5.8 constant_dynamic-update-slice_fusion.9
  350.6 6.0 constant_dynamic-update-slice_fusion.8
  358.4 3.2 constant_dynamic-update-slice_fusion.7
  364.6 24.6 %core_bwd.1 = (f32[1,256,512]{2,1,0:T(8,128)}, f32[1,256,512]{2,1,0:T(8,128)}, f32[1,256,1024]{2,1,0:T(8,128)}, f32[1,4,256,2]{3,2,1,0:T(8,128)}, f32[1,4,1,256]{3,2,1,0:T(1,128)}) custom-call(s32[1]{0:T(128)} %bitcast.1.place_ref, bf16[4,1,4,128,384]{4,3,2,1,0:T(8,128)(2,1)} %bitcast.174, bf16[4,1,4,128,256]{4,3,2,1,0:T(8,128)(2,1)} %bitcast.195, ...), custom_call_target="tpu_custom_call" | custom-call | flops 8053063680 | bytes 13656068 | tf_op jit(solution)/shard_map/core_bwd/pallas_call | solution.py:213
  392.8 5.5 multiply_reduce_fusion.2
  421.9 4.8 fusion.50
  427.0 5.8 multiply_reduce_fusion.5
  433.7 3.6 fusion.46
  443.9 5.4 fusion.5
  450.6 104.1 %all-reduce.13.cloned.1.call-done = f32[152,128]{1,0:T(8,128)} async-done(((f32[152,128]{1,0:T(8,128)}), f32[152,128]{1,0:T(8,128)}) %all-reduce.13.cloned.1.call-update) | async-done | bytes 77840 | tf_op jit(solution)/shard_map/psum | solution.py:434
  559.6 548.6 %reduce-scatter.2.cloned.1.call-done = bf16[392,1024]{1,0:T(8,128)(2,1)} async-done(((bf16[12544,1024]{1,0:T(8,128)(2,1)}), bf16[392,1024]{1,0:T(8,128)(2,1)}) %reduce-scatter.2.cloned.1.call-update) | async-done | bytes 802832 | tf_op jit(solution)/shard_map/reduce_scatter | solution.py:270
  (163 shorter events, 75.0 us)
Async XLA Ops:
  7.2 77.3 %all-gather.7.cloned.1.call-start = ((), (), s32[]{:S(2)}) async-start(), calls=%async_computation.1 | async-start | bytes 6758400 | tf_op jit(solution)/shard_map/all_gather | solution.py:254
  9.7 165.2 %all-gather.11.cloned.1.call-start = ((), (), s32[]{:S(2)}) async-start(), calls=%async_computation.5 | async-start | bytes 1966080 | tf_op jit(solution)/shard_map/all_gather | solution.py:335
  11.8 82.2 %copy-start.36 = (f32[4]{0:T(128)}, f32[4]{0:T(128)S(1)}, u32[]{:S(2)}) copy-start(f32[4]{0:T(128)S(1)} %exponential_negate_fusion) | copy-start | bytes 52
  11.8 77.9 %copy-start.29 = (f32[256]{0:T(256)}, f32[256]{0:T(256)S(1)}, u32[]{:S(2)}) copy-start(f32[256]{0:T(256)S(1)} %add_rsqrt_fusion.1) | copy-start | bytes 3076
  12.8 81.3 %copy-start.35 = (f32[4]{0:T(128)S(1)}, f32[4]{0:T(128)}, u32[]{:S(2)}) copy-start(f32[4]{0:T(128)} %param.21) | copy-start | bytes 52
  89.7 6.4 copy-start
  90.6 6.9 collective-permute-start
  103.9 36.3 %copy-start.23 = (bf16[2,88,1024]{2,1,0:T(8,128)(2,1)S(1)}, bf16[2,88,1024]{2,1,0:T(8,128)(2,1)}, u32[]{:S(2)}) copy-start(bf16[2,88,1024]{2,1,0:T(8,128)(2,1)} %param.25) | copy-start | bytes 1081348
  103.9 36.4 %copy-start.25 = (bf16[88,1024]{1,0:T(8,128)(2,1)S(1)}, bf16[88,1024]{1,0:T(8,128)(2,1)}, u32[]{:S(2)}) copy-start(bf16[88,1024]{1,0:T(8,128)(2,1)} %param.26) | copy-start | bytes 540676
  103.9 36.4 %copy-start.27 = (bf16[32,1024]{1,0:T(8,128)(2,1)S(1)}, bf16[32,1024]{1,0:T(8,128)(2,1)}, u32[]{:S(2)}) copy-start(bf16[32,1024]{1,0:T(8,128)(2,1)} %param.23) | copy-start | bytes 196612
  140.2 163.3 %all-gather.9.cloned.1.call-start = ((), (), s32[]{:S(2)}) async-start(), calls=%async_computation.2 | async-start | bytes 20004864 | tf_op jit(solution)/shard_map/all_gather | solution.py:254
  141.2 223.4 %all-gather.13.cloned.1.call-start = ((), (), s32[]{:S(2)}) async-start(), calls=%async_computation.6 | async-start | bytes 1310720 | tf_op jit(solution)/shard_map/all_gather | solution.py:384
  305.3 7.4 copy-start.8
  305.3 7.4 copy-start.20
  313.6 16.3 %copy-start.12 = (f32[256,1024]{1,0:T(8,128)}, f32[256,1024]{1,0:T(8,128)S(1)}, u32[]{:S(2)}) copy-start(f32[256,1024]{1,0:T(8,128)S(1)} %get-tuple-element.139) | copy-start | bytes 3145732
  330.2 31.3 %copy-start.10 = (f32[256,1024]{1,0:T(8,128)}, f32[256,1024]{1,0:T(8,128)S(1)}, u32[]{:S(2)}) copy-start(f32[256,1024]{1,0:T(8,128)S(1)} %bitcast_add_fusion) | copy-start | bytes 3145732
  338.2 216.6 %all-reduce.13.cloned.1.call-start = ((), (), s32[]{:S(2)}) async-start(), calls=%async_computation.3 | async-start | bytes 155648 | tf_op jit(solution)/shard_map/psum | solution.py:434
  350.6 6.0 copy-start.19
  408.3 8.6 copy-start.3
  408.3 8.6 copy-start.5
  410.9 6.0 collective-permute-start.1
  427.0 5.8 copy-start.31
  427.0 5.8 copy-start.32
  433.6 674.5 %reduce-scatter.2.cloned.1.call-start = ((), (), s32[]{:S(2)}) async-start(), calls=%async_computation.4 | async-start | bytes 26492928 | tf_op jit(solution)/shard_map/reduce_scatter | solution.py:270
  (22 other events, 77.4 us)
Sparse Core Ops, SparseCore 0:
  11.4 73.0 all-gather.6
  140.3 34.5 all-gather.10
  178.4 125.1 all-gather.8
  338.3 26.2 all-gather.12
  433.7 120.9 all-reduce.12
  556.9 551.2 reduce-scatter.1
